TPU v7x, 32 devices: a whole 2x2x4 slice. The times are simulated.
32 devices in a mesh: wide: 8 (over y, x, core), narrow: 4 (over z).
Axes of the slice: x: 2, y: 2, z: 4, core: 2. Of those that a mesh axis runs over, the one named last changes fastest.
Arguments:
- tokens: bfloat16 [32, 512, 256], P('wide', 'narrow'), may hold values from -6 to 6
- kind: int32 [32], P('wide'), may hold values from 0 to 1
- proj_weight: bfloat16 [2, 256, 768], replicated, may hold values from -0.375 to 0.375
- proj_bias: float32 [2, 768], replicated, may hold values from -1.8 to 1.8
- ln1_gain: float32 [768], replicated, may hold values from 0.5 to 1.5
- ln1_bias: float32 [768], replicated, may hold values from -1.2 to 1.2
- qkv_weight: bfloat16 [768, 3, 768], P(None, None, 'narrow'), may hold values from -0.21875 to 0.21875
- qv_bias: float32 [2, 768], P(None, 'narrow'), may hold values from -1.8 to 1.8
- out_weight: bfloat16 [768, 768], P('narrow'), may hold values from -0.75 to 0.75
- out_bias: float32 [768], replicated, may hold values from -1.2 to 1.2
- ln2_gain: float32 [768], replicated, may hold values from 0.5 to 1.5
- ln2_bias: float32 [768], replicated, may hold values from -1.2 to 1.2
- up_weight: bfloat16 [768, 3072], P(None, 'narrow'), may hold values from -0.21875 to 0.21875
- up_bias: float32 [3072], replicated, may hold values from -1.8 to 1.8
- down_weight: bfloat16 [3072, 768], P('narrow'), may hold values from -0.109375 to 0.109375
- down_bias: float32 [768], replicated, may hold values from -1.2 to 1.2
- cotangent: bfloat16 [32, 512, 768], P('wide', 'narrow'), may hold values from -6 to 6
Outputs:
- out: bfloat16 [32, 512, 768], P('wide', 'narrow')
- tokens_grad: float32 [32, 512, 256], P('wide', 'narrow')
- proj_weight_grad: float32 [2, 256, 768], replicated
- proj_bias_grad: float32 [2, 768], replicated
- ln1_gain_grad: float32 [768], replicated
- ln1_bias_grad: float32 [768], replicated
- qkv_weight_grad: float32 [768, 3, 768], P(None, None, 'narrow')
- qv_bias_grad: float32 [2, 768], P(None, 'narrow')
- out_weight_grad: float32 [768, 768], P('narrow')
- out_bias_grad: float32 [768], replicated
- ln2_gain_grad: float32 [768], replicated
- ln2_bias_grad: float32 [768], replicated
- up_weight_grad: float32 [768, 3072], P(None, 'narrow')
- up_bias_grad: float32 [3072], P('narrow')
- down_weight_grad: float32 [3072, 768], P('narrow')
- down_bias_grad: float32 [768], replicated
Inputs may be any that keep to these rules, and one draw needn't show every extreme that they name: kind[c] is 0 for a clip of frame tokens and 1 for a clip of patch tokens.
All inputs are finite; a program needn't handle non-finite values.
Results may differ from a plain program's by a relative error of at most 0.019.
Values may be sent and summed in bfloat16 or wider, within the bound.
No kernel may reach another device: no remote copies, remote signals or barrier semaphores. Data moves between devices by JAX's collectives and lax.ppermute only.
A program may use at most 192 MiB of HBM per device.

v0:
```python
import jax
import jax.numpy as jnp
from jax import lax
from jax.sharding import PartitionSpec as P

HEAD_DIM = 64
epsilon = 1e-06


def layer_norm(values, norm_gain, norm_shift):
    row_mean = jnp.mean(values, axis=-1, keepdims=True)
    centred = values - row_mean
    row_var = jnp.mean(centred * centred, axis=-1, keepdims=True)
    return centred * lax.rsqrt(row_var + epsilon) * norm_gain + norm_shift


def exact_gelu(values):
    return 0.5 * values * (1.0 + jax.scipy.special.erf(values * 2.0 ** (-0.5)))


def project_heads(rows_full, qkv_weight, qv_bias):
    zero_row = jnp.zeros_like(qv_bias[0])
    bias_three = jnp.stack([qv_bias[0], zero_row, qv_bias[1]])
    projected = jnp.einsum(
        "cld,dke->kcle", rows_full, qkv_weight, preferred_element_type=jnp.float32
    )
    projected = (projected + bias_three[:, None, None, :]).astype(jnp.bfloat16)
    head_count = projected.shape[3] // HEAD_DIM
    return projected.reshape(3, projected.shape[1], projected.shape[2], head_count, HEAD_DIM)


def score_block(heads_qkv):
    return jnp.einsum(
        "clhe,cmhe->chlm", heads_qkv[0], heads_qkv[1], preferred_element_type=jnp.float32
    ) * HEAD_DIM ** (-0.5)


def mix_values(probs_low, heads_qkv):
    mixed = jnp.einsum(
        "chlm,cmhe->clhe", probs_low, heads_qkv[2], preferred_element_type=jnp.float32
    )
    mixed = mixed.astype(jnp.bfloat16)
    return mixed.reshape(mixed.shape[0], mixed.shape[1], mixed.shape[2] * mixed.shape[3])


def ffn_backward(rows_in, grad_rows, weight_in, weight_out, bias_in):
    hidden_pre = (
        jnp.einsum("cld,df->clf", rows_in, weight_in, preferred_element_type=jnp.float32) + bias_in
    )
    hidden_back = exact_gelu(hidden_pre).astype(jnp.bfloat16)
    out_grad = jnp.einsum("clf,cld->fd", hidden_back, grad_rows, preferred_element_type=jnp.float32)
    hidden_grad = jnp.einsum(
        "cld,fd->clf", grad_rows, weight_out, preferred_element_type=jnp.float32
    )
    gelu_value, gelu_pull = jax.vjp(exact_gelu, hidden_pre)
    pre_grad = gelu_pull(hidden_grad)[0].astype(jnp.bfloat16)
    in_grad = jnp.einsum("cld,clf->df", rows_in, pre_grad, preferred_element_type=jnp.float32)
    in_bias_grad = jnp.sum(pre_grad, axis=(0, 1), dtype=jnp.float32)
    rows_grad = jnp.einsum("clf,df->cld", pre_grad, weight_in, preferred_element_type=jnp.float32)
    return (in_grad, in_bias_grad, out_grad, rows_grad)


def per_device(
    tokens,
    kind,
    proj_weight,
    proj_bias,
    ln1_gain,
    ln1_bias,
    qkv_weight,
    qv_bias,
    out_weight,
    out_bias,
    ln2_gain,
    ln2_bias,
    up_weight,
    up_bias,
    down_weight,
    down_bias,
    cotangent,
):
    unit_share = up_weight.shape[1]
    local_bias = lax.dynamic_slice_in_dim(
        up_bias, lax.axis_index("narrow") * unit_share, unit_share, 0
    )
    is_patch = kind == 1
    chosen = jnp.where(is_patch[:, None, None], proj_weight[1], proj_weight[0])
    chosen_bias = jnp.where(is_patch[:, None], proj_bias[1], proj_bias[0])
    start_rows = (
        jnp.einsum("clf,cfd->cld", tokens, chosen, preferred_element_type=jnp.float32)
        + chosen_bias[:, None, :]
    )
    normed_one = layer_norm(start_rows, ln1_gain, ln1_bias).astype(jnp.bfloat16)
    rows_one = lax.all_gather(normed_one, "narrow", axis=1, tiled=True)
    heads_qkv = project_heads(rows_one, qkv_weight, qv_bias)
    scores = score_block(heads_qkv)
    row_max = jnp.max(scores, axis=-1, keepdims=True)
    log_total = row_max + jnp.log(jnp.sum(jnp.exp(scores - row_max), axis=-1, keepdims=True))
    probs_low = jnp.exp(scores - log_total).astype(jnp.bfloat16)
    mixed = mix_values(probs_low, heads_qkv)
    attn_part = jnp.einsum("cle,ed->cld", mixed, out_weight, preferred_element_type=jnp.float32)
    attn_rows = lax.psum_scatter(
        attn_part.astype(jnp.bfloat16), "narrow", scatter_dimension=1, tiled=True
    ).astype(jnp.float32)
    middle = start_rows + attn_rows + out_bias
    normed_two = layer_norm(middle, ln2_gain, ln2_bias).astype(jnp.bfloat16)
    rows_two = lax.all_gather(normed_two, "narrow", axis=1, tiled=True)
    hidden = exact_gelu(
        jnp.einsum("cld,df->clf", rows_two, up_weight, preferred_element_type=jnp.float32)
        + local_bias
    ).astype(jnp.bfloat16)
    mlp_part = jnp.einsum("clf,fd->cld", hidden, down_weight, preferred_element_type=jnp.float32)
    mlp_rows = lax.psum_scatter(
        mlp_part.astype(jnp.bfloat16), "narrow", scatter_dimension=1, tiled=True
    ).astype(jnp.float32)
    final_rows = middle + mlp_rows + down_bias
    output = final_rows.astype(jnp.bfloat16)
    down_bias_grad = jnp.sum(cotangent, axis=(0, 1), dtype=jnp.float32)
    grad_all = lax.all_gather(cotangent, "narrow", axis=1, tiled=True)
    rows_two_back = lax.all_gather(normed_two, "narrow", axis=1, tiled=True)
    up_weight_grad, up_bias_grad, down_weight_grad, norm_two_part = ffn_backward(
        rows_two_back, grad_all, up_weight, down_weight, local_bias
    )
    norm_two_grad = lax.psum_scatter(
        norm_two_part.astype(jnp.bfloat16), "narrow", scatter_dimension=1, tiled=True
    ).astype(jnp.float32)
    ln_value, ln_pull = jax.vjp(layer_norm, middle, ln2_gain, ln2_bias)
    mid_grad, ln2_gain_grad, ln2_bias_grad = ln_pull(norm_two_grad)
    mid_grad = mid_grad + cotangent.astype(jnp.float32)
    mid_low = mid_grad.astype(jnp.bfloat16)
    out_bias_grad = jnp.sum(mid_low, axis=(0, 1), dtype=jnp.float32)
    mid_all = lax.all_gather(mid_low, "narrow", axis=1, tiled=True)
    rows_one_back = lax.all_gather(normed_one, "narrow", axis=1, tiled=True)
    heads_back = project_heads(rows_one_back, qkv_weight, qv_bias)
    probs = jnp.exp(score_block(heads_back) - log_total)
    probs_back = probs.astype(jnp.bfloat16)
    mixed_back = mix_values(probs_back, heads_back)
    out_weight_grad = jnp.einsum(
        "cle,cld->ed", mixed_back, mid_all, preferred_element_type=jnp.float32
    )
    mixed_grad = jnp.einsum("cld,ed->cle", mid_all, out_weight, preferred_element_type=jnp.float32)
    mixed_grad = mixed_grad.astype(jnp.bfloat16).reshape(heads_back.shape[1:])
    probs_grad = jnp.einsum(
        "clhe,cmhe->chlm", mixed_grad, heads_back[2], preferred_element_type=jnp.float32
    )
    value_grad = jnp.einsum(
        "chlm,clhe->cmhe", probs_back, mixed_grad, preferred_element_type=jnp.float32
    )
    score_grad = probs * (probs_grad - jnp.sum(probs * probs_grad, axis=-1, keepdims=True))
    score_grad = score_grad.astype(jnp.bfloat16)
    query_grad = jnp.einsum(
        "chlm,cmhe->clhe", score_grad, heads_back[1], preferred_element_type=jnp.float32
    ) * HEAD_DIM ** (-0.5)
    key_grad = jnp.einsum(
        "chlm,clhe->cmhe", score_grad, heads_back[0], preferred_element_type=jnp.float32
    ) * HEAD_DIM ** (-0.5)
    stacked = jnp.stack([query_grad, key_grad, value_grad]).astype(jnp.bfloat16)
    stacked = stacked.reshape(
        3, stacked.shape[1], stacked.shape[2], stacked.shape[3] * stacked.shape[4]
    )
    qkv_weight_grad = jnp.einsum(
        "cld,kcle->dke", rows_one_back, stacked, preferred_element_type=jnp.float32
    )
    qv_bias_grad = jnp.stack(
        [
            jnp.sum(stacked[0], axis=(0, 1), dtype=jnp.float32),
            jnp.sum(stacked[2], axis=(0, 1), dtype=jnp.float32),
        ]
    )
    norm_one_part = jnp.einsum(
        "kcle,dke->cld", stacked, qkv_weight, preferred_element_type=jnp.float32
    )
    norm_one_grad = lax.psum_scatter(
        norm_one_part.astype(jnp.bfloat16), "narrow", scatter_dimension=1, tiled=True
    ).astype(jnp.float32)
    first_value, first_pull = jax.vjp(layer_norm, start_rows, ln1_gain, ln1_bias)
    start_grad, ln1_gain_grad, ln1_bias_grad = first_pull(norm_one_grad)
    start_low = (start_grad + mid_grad).astype(jnp.bfloat16)
    tokens_grad = jnp.einsum("cld,cfd->clf", start_low, chosen, preferred_element_type=jnp.float32)
    per_clip = jnp.einsum("clf,cld->cfd", tokens, start_low, preferred_element_type=jnp.float32)
    clip_bias = jnp.sum(start_low, axis=1, dtype=jnp.float32)
    proj_weight_grad = jnp.stack(
        [
            jnp.sum(jnp.where(is_patch[:, None, None], 0.0, per_clip), axis=0),
            jnp.sum(jnp.where(is_patch[:, None, None], per_clip, 0.0), axis=0),
        ]
    )
    proj_bias_grad = jnp.stack(
        [
            jnp.sum(jnp.where(is_patch[:, None], 0.0, clip_bias), axis=0),
            jnp.sum(jnp.where(is_patch[:, None], clip_bias, 0.0), axis=0),
        ]
    )
    common = lax.psum(
        (
            proj_weight_grad,
            proj_bias_grad,
            ln1_gain_grad,
            ln1_bias_grad,
            out_bias_grad,
            ln2_gain_grad,
            ln2_bias_grad,
            down_bias_grad,
        ),
        ("wide", "narrow"),
    )
    summed = lax.psum(
        (
            qkv_weight_grad,
            qv_bias_grad,
            out_weight_grad,
            up_weight_grad,
            up_bias_grad,
            down_weight_grad,
        ),
        "wide",
    )
    qkv_sum, qv_sum, out_sum, up_sum, up_bias_sum, down_sum = summed
    return (
        output,
        tokens_grad,
        common[0],
        common[1],
        common[2],
        common[3],
        qkv_sum,
        qv_sum,
        out_sum,
        common[4],
        common[5],
        common[6],
        up_sum,
        up_bias_sum,
        down_sum,
        common[7],
    )


def solution(mesh):
    in_specs = (
        P("wide", "narrow", None),
        P("wide"),
        P(),
        P(),
        P(),
        P(),
        P(None, None, "narrow"),
        P(None, "narrow"),
        P("narrow", None),
        P(),
        P(),
        P(),
        P(None, "narrow"),
        P(),
        P("narrow", None),
        P(),
        P("wide", "narrow", None),
    )
    out_specs = (
        P("wide", "narrow", None),
        P("wide", "narrow", None),
        P(),
        P(),
        P(),
        P(),
        P(None, None, "narrow"),
        P(None, "narrow"),
        P("narrow", None),
        P(),
        P(),
        P(),
        P(None, "narrow"),
        P("narrow"),
        P("narrow", None),
        P(),
    )
    return jax.shard_map(
        per_device, mesh=mesh, in_specs=in_specs, out_specs=out_specs, check_vma=False
    )
```

profile of v0, /device:TPU:0, one launch (start us, length us, event | category | flops | bytes accessed | tf_op | source)
XLA Modules:
  0.0 846.0 jit_solution(3704368714855647152)
XLA Ops:
  10.1 2.2 bitcast_reduce_fusion
  15.4 66.1 %all-gather.5.cloned.1.call-done = bf16[4,512,768]{1,2,0:T(8,128)(2,1)} async-done(((bf16[4,128,768]{1,2,0:T(8,128)(2,1)}), bf16[4,512,768]{1,2,0:T(8,128)(2,1)}) %all-gather.5.cloned.1.call-update) | async-done | bytes 3145744 | tf_op jit(solution)/shard_map/all_gather | solution.py:94
  81.5 4.0 fusion.5
  87.5 2.1 exponential_reduce_fusion
  89.7 2.4 copy-done.2
  92.0 2.5 convolution_convert_fusion.5
  95.6 2.4 copy.95
  98.0 2.3 copy.107
  100.6 58.5 %reduce-scatter.13.cloned.1.call-done = bf16[128,3072]{1,0:T(8,128)(2,1)} async-done(((bf16[512,3072]{1,0:T(8,128)(2,1)}), bf16[128,3072]{1,0:T(8,128)(2,1)}) %reduce-scatter.13.cloned.1.call-update) | async-done | bytes 786448
  159.1 2.0 reshape.196
  169.0 61.4 %all-gather.7.cloned.1.call-done = bf16[4,512,768]{1,2,0:T(8,128)(2,1)} async-done(((bf16[4,128,768]{1,2,0:T(8,128)(2,1)}), bf16[4,512,768]{1,2,0:T(8,128)(2,1)}) %all-gather.7.cloned.1.call-update) | async-done | bytes 3145744 | tf_op jit(solution)/shard_map/all_gather | solution.py:107
  230.4 7.5 multiply_convert_fusion.1
  237.9 55.6 %all-gather.9.cloned.1.call-done = bf16[4,512,768]{2,1,0:T(8,128)(2,1)} async-done(((bf16[4,128,768]{2,1,0:T(8,128)(2,1)}), bf16[4,512,768]{2,1,0:T(8,128)(2,1)}) %all-gather.9.cloned.1.call-update) | async-done | bytes 3145744 | tf_op jit(solution)/shard_map/all_gather | solution.py:119
  293.5 8.1 convert_reduce_fusion
  303.3 2.9 convolution_convert_fusion.1
  306.1 2.4 copy.99
  308.6 2.4 copy.109
  313.3 56.9 %reduce-scatter.17.cloned.1.call-done = bf16[128,3072]{1,0:T(8,128)(2,1)} async-done(((bf16[512,3072]{1,0:T(8,128)(2,1)}), bf16[128,3072]{1,0:T(8,128)(2,1)}) %reduce-scatter.17.cloned.1.call-update) | async-done | bytes 786448
  370.2 2.7 reshape.200
  377.2 2.2 convert_reduce_fusion.6
  379.5 4.8 convolution_convert_fusion.2
  384.3 2.4 copy.97
  386.8 2.5 copy.108
  389.5 53.4 %all-gather.11.cloned.1.call-done = bf16[4,512,768]{1,2,0:T(8,128)(2,1)} async-done(((bf16[4,128,768]{1,2,0:T(8,128)(2,1)}), bf16[4,512,768]{1,2,0:T(8,128)(2,1)}) %all-gather.11.cloned.1.call-update) | async-done | bytes 3145744 | tf_op jit(solution)/shard_map/all_gather | solution.py:132
  442.9 2.7 convolution_convert_fusion.3
  445.6 10.6 %multiply_reduce_fusion = (f32[4,3,512]{2,1,0:T(4,128)S(1)}, f32[4,3,512,512]{2,3,1,0:T(8,128)}) fusion(f32[4,3,512,512]{2,3,1,0:T(8,128)} %copy-done.2, f32[4,3,512]{2,1,0:T(4,128)S(1)} %copy-done.23, bf16[4,512,3,64]{1,3,2,0:T(8,128)(2,1)S(1)} %bitcast.173, bf16[4,512,3,64]{1,3,2,0:T(8,128)(2,1)S(1)} %bitcast.160), kind=kOutput, calls=%fused_computation.1 | convolution fusion | flops 415229952 | bytes 26787840 | tf_op jit(solution)/shard_map/clhe,cmhe->chlm/dot_general | solution.py:143
  458.9 6.9 multiply_convert_fusion
  465.8 2.0 multiply_convert_fusion.2
  469.6 3.2 convert_reduce_fusion.4
  472.8 3.0 bitcast_convert_fusion
  475.8 2.4 copy.101
  478.2 2.3 copy.110
  480.8 7.1 convolution_bitcast_fusion
  487.9 4.0 convolution_bitcast_fusion.1
  491.9 11.9 %reduce-scatter.15.cloned.1.call-done = bf16[128,3072]{1,0:T(8,128)(2,1)} async-done(((bf16[512,3072]{1,0:T(8,128)(2,1)}), bf16[128,3072]{1,0:T(8,128)(2,1)}) %reduce-scatter.15.cloned.1.call-update) | async-done | bytes 786448
  507.2 59.3 %reduce-scatter.19.cloned.1.call-done = bf16[128,3072]{1,0:T(8,128)(2,1)} async-done(((bf16[512,3072]{1,0:T(8,128)(2,1)}), bf16[128,3072]{1,0:T(8,128)(2,1)}) %reduce-scatter.19.cloned.1.call-update) | async-done | bytes 786448
  566.5 2.7 reshape.202
  570.8 2.8 convert_reduce_fusion.1
  573.6 2.8 fusion.19
  576.5 3.5 convert_reduce_fusion.7
  582.2 4.0 convolution_bitcast_fusion.2
  586.3 5.3 fusion.23
  592.4 14.2 %all-reduce.1 = (f32[2,192]{1,0:T(2,128)}, f32[768]{0:T(1024)}) all-reduce(f32[2,192]{1,0:T(2,128)S(1)} %pad_maximum_fusion.6, f32[768]{0:T(1024)S(1)} %copy-done.57), channel_id=1, replica_groups=mesh['wide'=8,'narrow'=4] {'wide'}, use_global_device_ids=true, to_apply=%region_29.30 | all-reduce | flops 1152 | bytes 9216 | tf_op jit(solution)/shard_map/psum | solution.py:207
  608.0 41.0 %all-reduce = (f32[2,768]{1,0:T(2,128)}, f32[768]{0:T(1024)}, f32[768]{0:T(1024)}, f32[768]{0:T(1024)}, f32[768]{0:T(1024)}, /*index=5*/f32[768]{0:T(1024)}, f32[768]{0:T(1024)}) all-reduce(f32[2,768]{1,0:T(2,128)S(1)} %pad_maximum_fusion.4, f32[768]{0:T(1024)S(1)} %copy-done.49, ...), channel_id=1, replica_groups=mesh['wide'=8,'narrow'=4] {'wide','narrow'}, use_global_device_ids=true, to_apply=%region_21.22 | all-reduce | flops 6144 | bytes 49152 | tf_op jit(solution)/shard_map/psum | solution.py:194
  650.5 64.2 %all-reduce.6.cloned.1.call-done = f32[2,256,768]{1,2,0:T(8,128)} async-done(((f32[2,256,768]{1,2,0:T(8,128)}), f32[2,256,768]{1,2,0:T(8,128)}) %all-reduce.6.cloned.1.call-update) | async-done | bytes 1572880 | tf_op jit(solution)/shard_map/psum | solution.py:194
  714.7 3.0 copy.77
  717.7 113.3 %all-reduce.8.cloned.1.call-done = (f32[768,3,192]{0,2,1:T(8,128)}, f32[192,768]{1,0:T(8,128)}, f32[768,768]{1,0:T(8,128)}, f32[768,768]{1,0:T(8,128)}) async-done(((f32[768,3,192]{0,2,1:T(8,128)}, f32[192,768]{1,0:T(8,128)}, f32[768,768]{1,0:T(8,128)}, f32[768,768]{1,0:T(8,128)}), (f32[768,3,192]{0,2,1:T(8,128)}, f32[192,768]{1,0:T(8,128)}, f32[768,768]{1,0:T(8,128)}, ...) | async-done | bytes 7077904 | tf_op jit(solution)/shard_map/psum | solution.py:207
  831.0 2.9 copy.116
  (212 shorter events, 45.8 us)
Async XLA Ops:
  7.2 223.2 %copy-start = (bf16[768,768]{1,0:T(8,128)(2,1)S(1)}, bf16[768,768]{1,0:T(8,128)(2,1)}, u32[]{:S(2)}) copy-start(bf16[768,768]{1,0:T(8,128)(2,1)} %param.29) | copy-start | bytes 3538948
  7.2 74.3 %all-gather.5.cloned.1.call-start = ((), (), s32[]{:S(2)}) async-start(), calls=%async_computation.4 | async-start | bytes 3932160 | tf_op jit(solution)/shard_map/all_gather | solution.py:94
  8.0 4.3 copy-start.60
  10.1 3.9 copy-start.36
  10.1 3.9 copy-start.54
  12.3 69.2 %copy-start.64 = (bf16[768,3,192]{0,2,1:T(8,128)(2,1)S(1)}, bf16[768,3,192]{0,2,1:T(8,128)(2,1)}, u32[]{:S(2)}) copy-start(bf16[768,3,192]{0,2,1:T(8,128)(2,1)} %param.23) | copy-start | bytes 2654212
  15.2 143.9 %reduce-scatter.13.cloned.1.call-start = ((), (), s32[]{:S(2)}) async-start(), calls=%async_computation.9 | async-start | bytes 3932160
  87.5 4.5 copy-start.2
  89.6 4.9 copy-start.22
  100.4 62.1 %copy-start.58 = (f32[768]{0:T(1024)S(1)}, f32[768]{0:T(1024)}, u32[]{:S(2)}) copy-start(f32[768]{0:T(1024)} %param.26) | copy-start | bytes 9220
  100.4 130.0 %all-gather.7.cloned.1.call-start = ((), (), s32[]{:S(2)}) async-start(), calls=%async_computation.5 | async-start | bytes 3932160 | tf_op jit(solution)/shard_map/all_gather | solution.py:107
  167.0 126.5 %all-gather.9.cloned.1.call-start = ((), (), s32[]{:S(2)}) async-start(), calls=%async_computation.6 | async-start | bytes 3932160 | tf_op jit(solution)/shard_map/all_gather | solution.py:119
  167.5 202.7 %reduce-scatter.17.cloned.1.call-start = ((), (), s32[]{:S(2)}) async-start(), calls=%async_computation.11 | async-start | bytes 3932160
  311.0 131.9 %all-gather.11.cloned.1.call-start = ((), (), s32[]{:S(2)}) async-start(), calls=%async_computation.7 | async-start | bytes 3932160 | tf_op jit(solution)/shard_map/all_gather | solution.py:132
  379.5 124.4 %reduce-scatter.15.cloned.1.call-start = ((), (), s32[]{:S(2)}) async-start(), calls=%async_computation.10 | async-start | bytes 3932160
  389.2 53.7 %copy-start.21 = (bf16[192,768]{1,0:T(8,128)(2,1)S(1)}, bf16[192,768]{1,0:T(8,128)(2,1)}, u32[]{:S(2)}) copy-start(bf16[192,768]{1,0:T(8,128)(2,1)} %param.25) | copy-start | bytes 884740
  389.3 56.3 %copy-start.23 = (f32[4,3,512]{2,1,0:T(4,128)S(1)}, f32[4,3,512]{2,1,0:T(4,128)}, u32[]{:S(2)}) copy-start(f32[4,3,512]{2,1,0:T(4,128)} %copy-done.22) | copy-start | bytes 73732
  389.3 177.2 %reduce-scatter.19.cloned.1.call-start = ((), (), s32[]{:S(2)}) async-start(), calls=%async_computation.12 | async-start | bytes 3932160
  445.6 10.7 %slice-start = ((s8[12582912]{0:T(1024)(128)(4,1)}), s8[4194304]{0:T(1024)(128)(4,1)S(1)}, s32[]{:S(2)}) async-start(s8[12582912]{0:T(1024)(128)(4,1)} %bitcast.157), calls=%async_computation.14 | async-start | bytes 8388608
  445.6 12.0 %slice-start.1 = ((s8[12582912]{0:T(1024)(128)(4,1)}), s8[4194304]{0:T(1024)(128)(4,1)S(1)}, s32[]{:S(2)}) async-start(s8[12582912]{0:T(1024)(128)(4,1)} %bitcast.157), calls=%async_computation.15 | async-start | bytes 8388608
  445.6 13.3 %slice-start.2 = ((s8[12582912]{0:T(1024)(128)(4,1)}), s8[4194304]{0:T(1024)(128)(4,1)S(1)}, s32[]{:S(2)}) async-start(s8[12582912]{0:T(1024)(128)(4,1)} %bitcast.157), calls=%async_computation.16 | async-start | bytes 8388608
  458.9 6.9 copy-start.6
  467.8 5.0 copy-start.18
  480.6 234.1 %all-reduce.6.cloned.1.call-start = ((), (), s32[]{:S(2)}) async-start(), calls=%async_computation.8 | async-start | bytes 3145728 | tf_op jit(solution)/shard_map/psum | solution.py:194
  480.8 7.1 copy-start.63
  480.8 7.1 copy-start.68
  569.2 4.4 copy-start.43
  569.2 4.4 copy-start.41
  570.7 5.7 copy-start.4
  570.8 5.7 copy-start.12
  570.8 5.7 copy-start.14
  570.8 5.7 copy-start.56
  582.1 4.2 copy-start.19
  582.1 4.1 copy-start.27
  582.1 4.1 copy-start.29
  582.1 248.9 %all-reduce.8.cloned.1.call-start = ((), (), s32[]{:S(2)}) async-start(), calls=%async_computation.13 | async-start | bytes 14155776 | tf_op jit(solution)/shard_map/psum | solution.py:207
  591.6 15.1 %copy-start.39 = (f32[4,768]{1,0:T(4,128)S(1)}, f32[4,768]{1,0:T(4,128)}, u32[]{:S(2)}) copy-start(f32[4,768]{1,0:T(4,128)} %get-tuple-element.77) | copy-start | bytes 36868
  591.6 15.1 %copy-start.62 = (pred[4]{0:T(512)(128)(4,1)S(1)}, pred[4]{0:T(512)(128)(4,1)}, u32[]{:S(2)}) copy-start(pred[4]{0:T(512)(128)(4,1)} %copy-done.60) | copy-start | bytes 16
  591.6 15.2 %copy-start.13 = (bf16[4,128,768]{1,2,0:T(8,128)(2,1)S(1)}, bf16[4,128,768]{1,2,0:T(8,128)(2,1)}, u32[]{:S(2)}) copy-start(bf16[4,128,768]{1,2,0:T(8,128)(2,1)} %get-tuple-element.84) | copy-start | bytes 2359300
  591.6 16.4 %copy-start.46 = (f32[768]{0:T(1024)S(1)}, f32[768]{0:T(1024)}, u32[]{:S(2)}) copy-start(f32[768]{0:T(1024)} %get-tuple-element.54) | copy-start | bytes 9220
  591.6 16.4 %copy-start.47 = (f32[768]{0:T(1024)S(1)}, f32[768]{0:T(1024)}, u32[]{:S(2)}) copy-start(f32[768]{0:T(1024)} %get-tuple-element.50) | copy-start | bytes 9220
  591.6 16.4 %copy-start.48 = (f32[768]{0:T(1024)S(1)}, f32[768]{0:T(1024)}, u32[]{:S(2)}) copy-start(f32[768]{0:T(1024)} %get-tuple-element.56) | copy-start | bytes 9220
  591.6 16.4 %copy-start.49 = (f32[768]{0:T(1024)S(1)}, f32[768]{0:T(1024)}, u32[]{:S(2)}) copy-start(f32[768]{0:T(1024)} %get-tuple-element.52) | copy-start | bytes 9220
  591.7 16.4 %copy-start.50 = (f32[768]{0:T(1024)S(1)}, f32[768]{0:T(1024)}, u32[]{:S(2)}) copy-start(f32[768]{0:T(1024)} %get-tuple-element.85) | copy-start | bytes 9220
  591.7 16.4 %copy-start.51 = (f32[768]{0:T(1024)S(1)}, f32[768]{0:T(1024)}, u32[]{:S(2)}) copy-start(f32[768]{0:T(1024)} %get-tuple-element.75) | copy-start | bytes 9220
  591.7 57.3 %copy-start.25 = (bf16[4,128,768]{1,2,0:T(8,128)(2,1)S(1)}, bf16[4,128,768]{1,2,0:T(8,128)(2,1)}, u32[]{:S(2)}) copy-start(bf16[4,128,768]{1,2,0:T(8,128)(2,1)} %copy-done.24) | copy-start | bytes 2359300
  591.7 57.3 %copy-start.32 = (bf16[256,768]{1,0:T(8,128)(2,1)S(1)}, bf16[256,768]{1,0:T(8,128)(2,1)}, u32[]{:S(2)}) copy-start(bf16[256,768]{1,0:T(8,128)(2,1)} %copy-done.31) | copy-start | bytes 1179652
  591.7 57.3 %copy-start.34 = (bf16[256,768]{1,0:T(8,128)(2,1)S(1)}, bf16[256,768]{1,0:T(8,128)(2,1)}, u32[]{:S(2)}) copy-start(bf16[256,768]{1,0:T(8,128)(2,1)} %copy-done.33) | copy-start | bytes 1179652
  (34 other events, 75.6 us)
Sparse Core Ops, SparseCore 0:
  15.3 66.1 all-gather.4
  100.5 58.5 reduce-scatter.12
  167.1 63.2 all-gather.6
  231.8 61.6 all-gather.8
  311.1 59.0 reduce-scatter.16
  379.6 63.2 all-gather.10
  445.2 58.5 reduce-scatter.14
  506.1 60.3 reduce-scatter.18
  582.2 132.4 all-reduce.5
  719.4 111.5 all-reduce.7
where the time goes:
time: 856 us; the launch traced here: 846 us
  waiting for transfers between devices  601 us (70%)
  matrix products  80.5 us (9%)
  local copies, waits for them, and re-layouts  62.2 us (7%)
  blocking collectives  55.2 us (6%)
  other arithmetic  29.9 us (3%)
  between operations  15.4 us (2%)
    unnamed x14, waiting for transfers between devices  187 us
    psum x1, waiting for transfers between devices, per_device(): lax.psum((qkv_weight_grad, qv_bias_grad, out_weight_grad, up_weight_grad,...  113 us
    all_gather x1, waiting for transfers between devices, per_device(): rows_one = lax.all_gather(normed_one, 'narrow', axis=1, tiled=True)  66.1 us
    psum x1, waiting for transfers between devices, per_device(): lax.psum((proj_weight_grad, proj_bias_grad, ln1_gain_grad, ln1_bias_grad,...  64.2 us
    all_gather x1, waiting for transfers between devices, per_device(): rows_two = lax.all_gather(normed_two, 'narrow', axis=1, tiled=True)  61.4 us
    unnamed x167, local copies, waits for them, and re-layouts  58.5 us
    all_gather x1, waiting for transfers between devices, per_device(): grad_all = lax.all_gather(cotangent, 'narrow', axis=1, tiled=True)  55.6 us
    all_gather x1, waiting for transfers between devices, per_device(): mid_all = lax.all_gather(mid_low, 'narrow', axis=1, tiled=True)  53.4 us
  transfers between devices with their start and end apart: 10, of which 10 were waited for; matrix products, arithmetic and copies ran while one was open for 10% of the time, Pallas kernels for 0%

commit v1 on v0

--- a/solution.py
+++ b/solution.py
@@ -116,8 +116,13 @@
     final_rows = middle + mlp_rows + down_bias
     output = final_rows.astype(jnp.bfloat16)
     down_bias_grad = jnp.sum(cotangent, axis=(0, 1), dtype=jnp.float32)
-    grad_all = lax.all_gather(cotangent, "narrow", axis=1, tiled=True)
-    rows_two_back = lax.all_gather(normed_two, "narrow", axis=1, tiled=True)
+    grad_all, rows_two_back = jnp.split(
+        lax.all_gather(
+            jnp.concatenate([cotangent, normed_two], axis=0), "narrow", axis=1, tiled=True
+        ),
+        [cotangent.shape[0]],
+        axis=0,
+    )
     up_weight_grad, up_bias_grad, down_weight_grad, norm_two_part = ffn_backward(
         rows_two_back, grad_all, up_weight, down_weight, local_bias
     )

time: 856 us -> 906 us (1.058)
  waiting for transfers between devices: 601 us -> 644 us
    all_gather x1, waiting for transfers between devices: 55.6 us -> 114 us  [per_device(): lax.all_gather(jnp.concatenate([cotangent, normed_two], axis=0), 'narrow'...]
    unnamed x167 -> x187, local copies, waits for them, and re-layouts: 58.5 us -> 58.7 us
  transfers between devices with their start and end apart: 10 -> 10, of which waited for: 10 -> 10; matrix products, arithmetic and copies ran while one was open for 10% -> 11% of each run, Pallas kernels for 0% -> 0%
where the time goes in v1:
time: 906 us; the launch traced here: 895 us
  waiting for transfers between devices  644 us (71%)
  matrix products  84.5 us (9%)
  local copies, waits for them, and re-layouts  61.9 us (7%)
  blocking collectives  54.8 us (6%)
  other arithmetic  33.6 us (4%)
  between operations  15.5 us (2%)
    unnamed x14, waiting for transfers between devices  183 us
    all_gather x1, waiting for transfers between devices, per_device(): lax.all_gather(jnp.concatenate([cotangent, normed_two], axis=0), 'narrow'...  114 us
    psum x1, waiting for transfers between devices, per_device(): lax.psum((qkv_weight_grad, qv_bias_grad, out_weight_grad, up_weight_grad,...  113 us
    all_gather x1, waiting for transfers between devices, per_device(): rows_one = lax.all_gather(normed_one, 'narrow', axis=1, tiled=True)  66.1 us
    psum x1, waiting for transfers between devices, per_device(): lax.psum((proj_weight_grad, proj_bias_grad, ln1_gain_grad, ln1_bias_grad,...  64.8 us
    unnamed x187, local copies, waits for them, and re-layouts  58.7 us
    all_gather x1, waiting for transfers between devices, per_device(): rows_two = lax.all_gather(normed_two, 'narrow', axis=1, tiled=True)  54.7 us
    all_gather x1, waiting for transfers between devices, per_device(): mid_all = lax.all_gather(mid_low, 'narrow', axis=1, tiled=True)  47.4 us
  transfers between devices with their start and end apart: 10, of which 10 were waited for; matrix products, arithmetic and copies ran while one was open for 11% of the time, Pallas kernels for 0%

profile of v1, /device:TPU:0, one launch (start us, length us, event | category | flops | bytes accessed | tf_op | source)
XLA Modules:
  0.0 895.4 jit_solution(4802723561751425792)
XLA Ops:
  10.1 2.2 bitcast_reduce_fusion
  15.4 66.1 %all-gather.5.cloned.1.call-done = bf16[4,512,768]{1,2,0:T(8,128)(2,1)} async-done(((bf16[4,128,768]{1,2,0:T(8,128)(2,1)}), bf16[4,512,768]{1,2,0:T(8,128)(2,1)}) %all-gather.5.cloned.1.call-update) | async-done | bytes 3145744 | tf_op jit(solution)/shard_map/all_gather | solution.py:94
  81.5 4.0 fusion.10
  87.5 2.1 exponential_reduce_fusion
  89.7 2.4 copy-done.2
  92.0 2.4 convolution_convert_fusion.4
  96.4 2.4 copy.106
  98.9 2.3 copy.118
  102.7 57.3 %reduce-scatter.13.cloned.1.call-done = bf16[128,3072]{1,0:T(8,128)(2,1)} async-done(((bf16[512,3072]{1,0:T(8,128)(2,1)}), bf16[128,3072]{1,0:T(8,128)(2,1)}) %reduce-scatter.13.cloned.1.call-update) | async-done | bytes 786448
  167.8 2.4 pad_maximum_fusion.1
  171.0 114.0 %all-gather.9.cloned.1.call-done = bf16[8,512,768]{1,2,0:T(8,128)(2,1)} async-done(((bf16[8,128,768]{1,2,0:T(8,128)(2,1)}), bf16[8,512,768]{1,2,0:T(8,128)(2,1)}) %all-gather.9.cloned.1.call-update) | async-done | bytes 6291472 | tf_op jit(solution)/shard_map/all_gather | solution.py:120
  285.1 4.8 fusion.43
  289.9 7.0 convert_reduce_fusion
  296.9 2.9 convolution_convert_fusion.1
  299.7 2.4 copy.110
  302.2 2.4 copy.120
  305.6 57.7 %reduce-scatter.17.cloned.1.call-done = bf16[128,3072]{1,0:T(8,128)(2,1)} async-done(((bf16[512,3072]{1,0:T(8,128)(2,1)}), bf16[128,3072]{1,0:T(8,128)(2,1)}) %reduce-scatter.17.cloned.1.call-update) | async-done | bytes 786448
  363.3 2.7 reshape.200
  369.5 2.1 fusion.27
  371.6 2.2 convert_reduce_fusion.6
  373.9 54.7 %all-gather.7.cloned.1.call-done = bf16[4,512,768]{1,2,0:T(8,128)(2,1)} async-done(((bf16[4,128,768]{1,2,0:T(8,128)(2,1)}), bf16[4,512,768]{1,2,0:T(8,128)(2,1)}) %all-gather.7.cloned.1.call-update) | async-done | bytes 3145744 | tf_op jit(solution)/shard_map/all_gather | solution.py:107
  428.6 9.3 %fusion.11 = bf16[4,512,768]{2,1,0:T(8,128)(2,1)} fusion(f32[768]{0:T(1024)} %copy-done.65, bf16[4,512,768]{1,2,0:T(8,128)(2,1)} %all-gather.7.cloned.1.call-done, bf16[768,768]{1,0:T(8,128)(2,1)} %param.31, bf16[768,768]{1,0:T(8,128)(2,1)S(1)} %copy-done), kind=kOutput, calls=%fused_computation.34 | convolution fusion | flops 4842848256 | bytes 8653824 | tf_op jit(solution)/shard_map/clf,fd->cld/dot_general | solution.py:112
  437.9 4.4 copy.108
  442.3 2.3 copy.119
  444.9 47.4 %all-gather.11.cloned.1.call-done = bf16[4,512,768]{1,2,0:T(8,128)(2,1)} async-done(((bf16[4,128,768]{1,2,0:T(8,128)(2,1)}), bf16[4,512,768]{1,2,0:T(8,128)(2,1)}) %all-gather.11.cloned.1.call-update) | async-done | bytes 3145744 | tf_op jit(solution)/shard_map/all_gather | solution.py:137
  492.3 2.7 convolution_convert_fusion.2
  495.0 10.6 %multiply_reduce_fusion = (f32[4,3,512]{2,1,0:T(4,128)S(1)}, f32[4,3,512,512]{2,3,1,0:T(8,128)}) fusion(f32[4,3,512,512]{2,3,1,0:T(8,128)} %copy-done.2, f32[4,3,512]{2,1,0:T(4,128)S(1)} %copy-done.25, bf16[4,512,3,64]{1,3,2,0:T(8,128)(2,1)S(1)} %bitcast.172, bf16[4,512,3,64]{1,3,2,0:T(8,128)(2,1)S(1)} %bitcast.159), kind=kOutput, calls=%fused_computation.1 | convolution fusion | flops 415229952 | bytes 26787840 | tf_op jit(solution)/shard_map/clhe,cmhe->chlm/dot_general | solution.py:148
  508.2 6.9 multiply_convert_fusion
  518.9 3.1 convert_reduce_fusion.4
  522.1 3.0 bitcast_convert_fusion
  525.1 2.4 copy.112
  527.5 2.3 copy.121
  530.1 6.8 convolution_bitcast_fusion
  537.0 7.7 fusion.22
  544.7 8.5 reduce-scatter.15.cloned.1.call-done
  556.5 59.3 %reduce-scatter.19.cloned.1.call-done = bf16[128,3072]{1,0:T(8,128)(2,1)} async-done(((bf16[512,3072]{1,0:T(8,128)(2,1)}), bf16[128,3072]{1,0:T(8,128)(2,1)}) %reduce-scatter.19.cloned.1.call-update) | async-done | bytes 786448
  615.8 2.7 reshape.202
  620.1 2.8 convert_reduce_fusion.1
  623.0 2.8 fusion.28
  625.8 3.5 convert_reduce_fusion.7
  631.6 4.0 convolution_bitcast_fusion.1
  635.6 5.3 fusion.32
  641.7 14.1 %all-reduce.1 = (f32[2,192]{1,0:T(2,128)}, f32[768]{0:T(1024)}) all-reduce(f32[2,192]{1,0:T(2,128)S(1)} %pad_maximum_fusion.7, f32[768]{0:T(1024)S(1)} %copy-done.64), channel_id=1, replica_groups=mesh['wide'=8,'narrow'=4] {'wide'}, use_global_device_ids=true, to_apply=%region_29.30 | all-reduce | flops 1152 | bytes 9216 | tf_op jit(solution)/shard_map/psum | solution.py:212
  657.2 40.7 %all-reduce = (f32[2,768]{1,0:T(2,128)}, f32[768]{0:T(1024)}, f32[768]{0:T(1024)}, f32[768]{0:T(1024)}, f32[768]{0:T(1024)}, /*index=5*/f32[768]{0:T(1024)}, f32[768]{0:T(1024)}) all-reduce(f32[2,768]{1,0:T(2,128)S(1)} %pad_maximum_fusion.5, f32[768]{0:T(1024)S(1)} %copy-done.56, ...), channel_id=1, replica_groups=mesh['wide'=8,'narrow'=4] {'wide','narrow'}, use_global_device_ids=true, to_apply=%region_21.22 | all-reduce | flops 6144 | bytes 49152 | tf_op jit(solution)/shard_map/psum | solution.py:199
  699.4 64.8 %all-reduce.6.cloned.1.call-done = f32[2,256,768]{1,2,0:T(8,128)} async-done(((f32[2,256,768]{1,2,0:T(8,128)}), f32[2,256,768]{1,2,0:T(8,128)}) %all-reduce.6.cloned.1.call-update) | async-done | bytes 1572880 | tf_op jit(solution)/shard_map/psum | solution.py:199
  764.2 3.0 copy.85
  767.2 113.3 %all-reduce.8.cloned.1.call-done = (f32[768,3,192]{0,2,1:T(8,128)}, f32[192,768]{1,0:T(8,128)}, f32[768,768]{1,0:T(8,128)}, f32[768,768]{1,0:T(8,128)}) async-done(((f32[768,3,192]{0,2,1:T(8,128)}, f32[192,768]{1,0:T(8,128)}, f32[768,768]{1,0:T(8,128)}, f32[768,768]{1,0:T(8,128)}), (f32[768,3,192]{0,2,1:T(8,128)}, f32[192,768]{1,0:T(8,128)}, f32[768,768]{1,0:T(8,128)}, ...) | async-done | bytes 7077904 | tf_op jit(solution)/shard_map/psum | solution.py:212
  880.5 2.9 copy.127
  (233 shorter events, 47.0 us)
Async XLA Ops:
  7.2 277.9 %copy-start = (bf16[768,768]{1,0:T(8,128)(2,1)S(1)}, bf16[768,768]{1,0:T(8,128)(2,1)}, u32[]{:S(2)}) copy-start(bf16[768,768]{1,0:T(8,128)(2,1)} %param.29) | copy-start | bytes 3538948
  7.2 74.3 %all-gather.5.cloned.1.call-start = ((), (), s32[]{:S(2)}) async-start(), calls=%async_computation.4 | async-start | bytes 3932160 | tf_op jit(solution)/shard_map/all_gather | solution.py:94
  12.3 69.2 %copy-start.74 = (bf16[768,3,192]{0,2,1:T(8,128)(2,1)S(1)}, bf16[768,3,192]{0,2,1:T(8,128)(2,1)}, u32[]{:S(2)}) copy-start(bf16[768,3,192]{0,2,1:T(8,128)(2,1)} %param.23) | copy-start | bytes 2654212
  15.2 144.7 %reduce-scatter.13.cloned.1.call-start = ((), (), s32[]{:S(2)}) async-start(), calls=%async_computation.9 | async-start | bytes 3932160
  87.5 4.5 copy-start.2
  89.7 4.8 copy-start.24
  101.2 62.1 %copy-start.67 = (f32[768]{0:T(1024)S(1)}, f32[768]{0:T(1024)}, u32[]{:S(2)}) copy-start(f32[768]{0:T(1024)} %param.26) | copy-start | bytes 9220
  101.2 183.9 %all-gather.9.cloned.1.call-start = ((), (), s32[]{:S(2)}) async-start(), calls=%async_computation.6 | async-start | bytes 7864320 | tf_op jit(solution)/shard_map/all_gather | solution.py:120
  102.7 65.1 %copy-start.7 = (bf16[4,128,768]{1,2,0:T(8,128)(2,1)}, bf16[4,128,768]{1,2,0:T(8,128)(2,1)S(1)}, u32[]{:S(2)}) copy-start(bf16[4,128,768]{1,2,0:T(8,128)(2,1)S(1)} %copy.65) | copy-start | bytes 2359300
  170.2 193.1 %reduce-scatter.17.cloned.1.call-start = ((), (), s32[]{:S(2)}) async-start(), calls=%async_computation.11 | async-start | bytes 3932160
  171.0 118.8 %copy-start.65 = (f32[768]{0:T(1024)}, f32[768]{0:T(1024)S(1)}, u32[]{:S(2)}) copy-start(f32[768]{0:T(1024)S(1)} %dynamic_slice.3) | copy-start | bytes 9220
  285.1 4.8 copy-start.72
  285.1 4.8 copy-start.73
  289.9 7.0 copy-start.77
  304.6 124.1 %all-gather.7.cloned.1.call-start = ((), (), s32[]{:S(2)}) async-start(), calls=%async_computation.5 | async-start | bytes 3932160 | tf_op jit(solution)/shard_map/all_gather | solution.py:107
  305.2 187.1 %all-gather.11.cloned.1.call-start = ((), (), s32[]{:S(2)}) async-start(), calls=%async_computation.7 | async-start | bytes 3932160 | tf_op jit(solution)/shard_map/all_gather | solution.py:137
  373.9 179.3 %reduce-scatter.15.cloned.1.call-start = ((), (), s32[]{:S(2)}) async-start(), calls=%async_computation.10 | async-start | bytes 3932160
  444.6 47.6 %copy-start.23 = (bf16[192,768]{1,0:T(8,128)(2,1)S(1)}, bf16[192,768]{1,0:T(8,128)(2,1)}, u32[]{:S(2)}) copy-start(bf16[192,768]{1,0:T(8,128)(2,1)} %param.25) | copy-start | bytes 884740
  444.7 50.3 %copy-start.6 = (bf16[1,4,512,192]{2,3,0,1:T(8,128)(2,1)S(1)}, bf16[1,4,512,192]{2,3,0,1:T(8,128)(2,1)}, u32[]{:S(2)}) copy-start(bf16[1,4,512,192]{2,3,0,1:T(8,128)(2,1)} %copy-done.5) | copy-start | bytes 2359300
  444.7 50.3 %copy-start.25 = (f32[4,3,512]{2,1,0:T(4,128)S(1)}, f32[4,3,512]{2,1,0:T(4,128)}, u32[]{:S(2)}) copy-start(f32[4,3,512]{2,1,0:T(4,128)} %copy-done.24) | copy-start | bytes 73732
  444.7 171.1 %reduce-scatter.19.cloned.1.call-start = ((), (), s32[]{:S(2)}) async-start(), calls=%async_computation.12 | async-start | bytes 3932160
  494.9 10.7 %slice-start = ((s8[12582912]{0:T(1024)(128)(4,1)}), s8[4194304]{0:T(1024)(128)(4,1)S(1)}, s32[]{:S(2)}) async-start(s8[12582912]{0:T(1024)(128)(4,1)} %bitcast.156), calls=%async_computation.14 | async-start | bytes 8388608
  495.0 12.0 %slice-start.1 = ((s8[12582912]{0:T(1024)(128)(4,1)}), s8[4194304]{0:T(1024)(128)(4,1)S(1)}, s32[]{:S(2)}) async-start(s8[12582912]{0:T(1024)(128)(4,1)} %bitcast.156), calls=%async_computation.15 | async-start | bytes 8388608
  495.0 13.3 %slice-start.2 = ((s8[12582912]{0:T(1024)(128)(4,1)}), s8[4194304]{0:T(1024)(128)(4,1)S(1)}, s32[]{:S(2)}) async-start(s8[12582912]{0:T(1024)(128)(4,1)} %bitcast.156), calls=%async_computation.16 | async-start | bytes 8388608
  508.2 6.9 copy-start.11
  517.1 5.0 copy-start.20
  529.9 7.1 copy-start.66
  529.9 234.3 %all-reduce.6.cloned.1.call-start = ((), (), s32[]{:S(2)}) async-start(), calls=%async_computation.8 | async-start | bytes 3145728 | tf_op jit(solution)/shard_map/psum | solution.py:199
  620.1 5.7 copy-start.4
  620.1 5.7 copy-start.9
  620.1 5.7 copy-start.17
  620.1 5.7 copy-start.42
  620.1 5.7 copy-start.45
  620.1 5.7 copy-start.52
  620.1 5.7 copy-start.63
  631.5 249.0 %all-reduce.8.cloned.1.call-start = ((), (), s32[]{:S(2)}) async-start(), calls=%async_computation.13 | async-start | bytes 14155776 | tf_op jit(solution)/shard_map/psum | solution.py:212
  640.9 14.9 %copy-start.43 = (f32[4,768]{1,0:T(4,128)S(1)}, f32[4,768]{1,0:T(4,128)}, u32[]{:S(2)}) copy-start(f32[4,768]{1,0:T(4,128)} %get-tuple-element.77) | copy-start | bytes 36868
  640.9 14.9 %copy-start.71 = (pred[4]{0:T(512)(128)(4,1)S(1)}, pred[4]{0:T(512)(128)(4,1)}, u32[]{:S(2)}) copy-start(pred[4]{0:T(512)(128)(4,1)} %copy-done.69) | copy-start | bytes 16
  640.9 15.0 %copy-start.16 = (bf16[4,128,768]{1,2,0:T(8,128)(2,1)S(1)}, bf16[4,128,768]{1,2,0:T(8,128)(2,1)}, u32[]{:S(2)}) copy-start(bf16[4,128,768]{1,2,0:T(8,128)(2,1)} %get-tuple-element.84) | copy-start | bytes 2359300
  641.0 16.2 %copy-start.53 = (f32[768]{0:T(1024)S(1)}, f32[768]{0:T(1024)}, u32[]{:S(2)}) copy-start(f32[768]{0:T(1024)} %get-tuple-element.54) | copy-start | bytes 9220
  641.0 16.2 %copy-start.54 = (f32[768]{0:T(1024)S(1)}, f32[768]{0:T(1024)}, u32[]{:S(2)}) copy-start(f32[768]{0:T(1024)} %get-tuple-element.50) | copy-start | bytes 9220
  641.0 16.2 %copy-start.55 = (f32[768]{0:T(1024)S(1)}, f32[768]{0:T(1024)}, u32[]{:S(2)}) copy-start(f32[768]{0:T(1024)} %get-tuple-element.56) | copy-start | bytes 9220
  641.0 16.2 %copy-start.56 = (f32[768]{0:T(1024)S(1)}, f32[768]{0:T(1024)}, u32[]{:S(2)}) copy-start(f32[768]{0:T(1024)} %get-tuple-element.52) | copy-start | bytes 9220
  641.0 16.2 %copy-start.57 = (f32[768]{0:T(1024)S(1)}, f32[768]{0:T(1024)}, u32[]{:S(2)}) copy-start(f32[768]{0:T(1024)} %get-tuple-element.85) | copy-start | bytes 9220
  641.0 16.2 %copy-start.58 = (f32[768]{0:T(1024)S(1)}, f32[768]{0:T(1024)}, u32[]{:S(2)}) copy-start(f32[768]{0:T(1024)} %get-tuple-element.75) | copy-start | bytes 9220
  641.0 56.9 %copy-start.27 = (bf16[4,128,768]{1,2,0:T(8,128)(2,1)S(1)}, bf16[4,128,768]{1,2,0:T(8,128)(2,1)}, u32[]{:S(2)}) copy-start(bf16[4,128,768]{1,2,0:T(8,128)(2,1)} %copy-done.26) | copy-start | bytes 2359300
  641.0 56.9 %copy-start.35 = (bf16[256,768]{1,0:T(8,128)(2,1)S(1)}, bf16[256,768]{1,0:T(8,128)(2,1)}, u32[]{:S(2)}) copy-start(bf16[256,768]{1,0:T(8,128)(2,1)} %copy-done.34) | copy-start | bytes 1179652
  641.0 56.8 %copy-start.37 = (bf16[256,768]{1,0:T(8,128)(2,1)S(1)}, bf16[256,768]{1,0:T(8,128)(2,1)}, u32[]{:S(2)}) copy-start(bf16[256,768]{1,0:T(8,128)(2,1)} %copy-done.36) | copy-start | bytes 1179652
  (44 other events, 118.6 us)
Sparse Core Ops, SparseCore 0:
  15.3 66.1 all-gather.4
  101.3 58.5 reduce-scatter.12
  170.3 114.7 all-gather.8
  304.7 58.5 reduce-scatter.16
  365.3 63.2 all-gather.6
  430.6 61.5 all-gather.10
  494.6 58.5 reduce-scatter.14
  555.5 60.2 reduce-scatter.18
  631.6 132.5 all-reduce.5
  768.9 111.5 all-reduce.7
